TPU v7x, 32 devices: a whole 2x2x4 slice. The times are simulated.
32 devices in a mesh: dp: 4 (over z), expert: 8 (over y, x, core).
Axes of the slice: x: 2, y: 2, z: 4, core: 2. Of those that a mesh axis runs over, the one named last changes fastest.
Arguments:
- block_input: bfloat16 [12608, 768], P(('dp', 'expert')), may hold values from -6 to 6
- out_grad: bfloat16 [12608, 768], P(('dp', 'expert')), may hold values from -6 to 6
- expert_ids: int32 [12608, 2], P(('dp', 'expert')), may hold values from 0 to 7, all different within a row
- slot_order: int32 [32, 394], P(('dp', 'expert')), may hold values from 0 to 393, each once within a row
- joint_weight: bfloat16 [768, 2304], P('expert'), may hold values from -0.21875 to 0.21875
- out_weight: bfloat16 [768, 768], P('expert'), may hold values from -0.625 to 0.625
- router_weight: bfloat16 [768, 8], P('expert'), may hold values from -0.4375 to 0.4375
- norm_gains: bfloat16 [2, 768], P(None, 'expert'), may hold values from 0.099609375 to 1.8984375
- norm_shifts: bfloat16 [2, 768], P(None, 'expert'), may hold values from -3 to 3
- attention_bias: bfloat16 [3, 768], P(None, 'expert'), may hold values from -3 to 3
- up_weight: bfloat16 [8, 768, 3072], P('expert'), may hold values from -0.21875 to 0.21875
- down_weight: bfloat16 [8, 3072, 768], P('expert'), may hold values from -3.5 to 3.5
- up_bias: bfloat16 [8, 3072], P('expert'), may hold values from -3 to 3
- down_bias: bfloat16 [8, 768], P('expert'), may hold values from -4 to 4
Outputs:
- block_output: bfloat16 [12608, 768], P(('dp', 'expert'))
- input_grad: bfloat16 [12608, 768], P(('dp', 'expert'))
- joint_grad: float32 [768, 2304], P('expert')
- out_weight_grad: float32 [768, 768], P('expert')
- router_grad: float32 [768, 8], P('expert')
- gains_grad: float32 [2, 768], P(None, 'expert')
- shifts_grad: float32 [2, 768], P(None, 'expert')
- attention_bias_grad: float32 [3, 768], P(None, 'expert')
- up_grad: float32 [8, 768, 3072], P('expert', None, 'dp')
- down_grad: float32 [8, 3072, 768], P('expert', 'dp')
- up_bias_grad: float32 [8, 3072], P('expert', 'dp')
- down_bias_grad: float32 [8, 768], P('expert', 'dp')
Inputs may be any that keep to these rules, and one draw needn't show every extreme that they name: `expert_ids`: the two experts of a token differ. `slot_order`: each row is a permutation of the 394 token positions of one device.
All inputs are finite; a program needn't handle non-finite values.
Results may differ from a plain program's by a relative error of at most 0.024.
Values may be sent and summed in bfloat16 or wider, within the bound.
No kernel may reach another device: no remote copies, remote signals or barrier semaphores. Data moves between devices by JAX's collectives and lax.ppermute only.
A program may use at most 192 MiB of HBM per device.

v0:
```python
import jax
import jax.numpy as jnp
from jax import lax
from jax.sharding import PartitionSpec as P

HEADS = 12
HEAD_DIM = 64
SEQ = 197
norm_eps = 1e-06


def layer_norm(values, gain_row, shift_row):
    row_mean = jnp.mean(values, axis=-1, keepdims=True)
    centered = values - row_mean
    row_var = jnp.mean(centered * centered, axis=-1, keepdims=True)
    return centered * lax.rsqrt(row_var + norm_eps) * gain_row + shift_row


def gelu_tanh(values):
    return jax.nn.gelu(values, approximate=True)


def slot_table(route_rows, order_row, expert_count, capacity):
    tokens_here = route_rows.shape[0]
    ordered = jnp.take(route_rows, order_row, axis=0)
    expert_iota = jnp.arange(expert_count, dtype=jnp.int32)
    first_hot = (ordered[:, 0:1] == expert_iota[None, :]).astype(jnp.int32)
    second_hot = (ordered[:, 1:2] == expert_iota[None, :]).astype(jnp.int32)
    first_slot = jnp.sum((jnp.cumsum(first_hot, axis=0) - first_hot) * first_hot, axis=1)
    second_base = jnp.sum(first_hot, axis=0, keepdims=True)
    second_slot = jnp.sum(
        (jnp.cumsum(second_hot, axis=0) - second_hot + second_base) * second_hot, axis=1
    )
    slot_rank = jnp.stack([first_slot, second_slot], axis=1)
    flat_rank = jnp.where(
        slot_rank < capacity, ordered * capacity + slot_rank, expert_count * capacity
    )
    token_flat = jnp.zeros((tokens_here, 2), jnp.int32).at[order_row].set(flat_rank)
    token_index = jnp.broadcast_to(
        jnp.arange(tokens_here, dtype=jnp.int32)[:, None], (tokens_here, 2)
    )
    source = (
        jnp.full((expert_count * capacity,), tokens_here, jnp.int32)
        .at[token_flat.reshape(-1)]
        .set(token_index.reshape(-1), mode="drop")
    )
    return (token_flat, source)


def per_device(
    block_input,
    out_grad,
    expert_ids,
    slot_order,
    joint_weight,
    out_weight,
    router_weight,
    norm_gains,
    norm_shifts,
    attention_bias,
    up_weight,
    down_weight,
    up_bias,
    down_bias,
):
    joint_full, out_full, router_full, gains_low, shifts_low, bias_low = (
        lax.all_gather(joint_weight, "expert", axis=0, tiled=True),
        lax.all_gather(out_weight, "expert", axis=0, tiled=True),
        lax.all_gather(router_weight, "expert", axis=0, tiled=True),
        lax.all_gather(norm_gains, "expert", axis=1, tiled=True),
        lax.all_gather(norm_shifts, "expert", axis=1, tiled=True),
        lax.all_gather(attention_bias, "expert", axis=1, tiled=True),
    )
    gains = gains_low.astype(jnp.float32)
    shifts = shifts_low.astype(jnp.float32)
    biases = bias_low.astype(jnp.float32)
    row_count, features = block_input.shape
    images = row_count // SEQ
    experts = router_full.shape[1]
    local_experts = up_weight.shape[0]
    capacity = max(2, (5 * row_count + 2 * experts - 1) // (2 * experts))
    head_scale = HEAD_DIM ** (-0.5)
    input_float = block_input.astype(jnp.float32)
    normed, norm_back = jax.vjp(layer_norm, input_float, gains[0], shifts[0])
    normed_low = normed.astype(jnp.bfloat16)
    joint_bias = jnp.concatenate([biases[0], jnp.zeros_like(biases[0]), biases[1]])
    projected = (
        jnp.dot(normed_low, joint_full, preferred_element_type=jnp.float32) + joint_bias
    ).astype(jnp.bfloat16)
    projected = projected.reshape(images, SEQ, 3, HEADS, HEAD_DIM)
    query_heads = projected[:, :, 0]
    key_heads = projected[:, :, 1]
    value_heads = projected[:, :, 2]
    scores = (
        jnp.einsum("ishd,ithd->ihst", query_heads, key_heads, preferred_element_type=jnp.float32)
        * head_scale
    )
    score_max = jnp.max(scores, axis=-1, keepdims=True)
    shifted = jnp.exp(scores - score_max)
    score_total = jnp.sum(shifted, axis=-1, keepdims=True)
    weighting = shifted / score_total
    log_total = score_max + jnp.log(score_total)
    attended = jnp.einsum(
        "ihst,ithd->ishd",
        weighting.astype(jnp.bfloat16),
        value_heads,
        preferred_element_type=jnp.float32,
    )
    attended_low = attended.reshape(row_count, features).astype(jnp.bfloat16)
    residual = (
        input_float
        + jnp.dot(attended_low, out_full, preferred_element_type=jnp.float32)
        + biases[2]
    )
    normed_two, norm_two_back = jax.vjp(layer_norm, residual, gains[1], shifts[1])
    two_low = normed_two.astype(jnp.bfloat16)
    logits = jnp.dot(two_low, router_full, preferred_element_type=jnp.float32)
    gate_weights = jax.nn.softmax(logits, axis=-1)
    chosen = jnp.take_along_axis(gate_weights, expert_ids, axis=1)
    token_flat, source = slot_table(expert_ids, slot_order[0], experts, capacity)
    dispatched = jnp.take(two_low, source, axis=0, mode="fill", fill_value=0).reshape(
        experts, capacity, features
    )
    arrived = lax.all_to_all(dispatched, "expert", split_axis=0, concat_axis=0, tiled=True)
    arrived_rows = arrived.reshape(-1, local_experts, capacity, features)
    pre_gelu = (
        jnp.einsum("secd,edf->secf", arrived_rows, up_weight, preferred_element_type=jnp.float32)
        + up_bias.astype(jnp.float32)[None, :, None, :]
    )
    hidden, gelu_back = jax.vjp(gelu_tanh, pre_gelu)
    hidden_low = hidden.astype(jnp.bfloat16)
    expert_out = (
        jnp.einsum("secf,efd->secd", hidden_low, down_weight, preferred_element_type=jnp.float32)
        + down_bias.astype(jnp.float32)[None, :, None, :]
    )
    expert_low = expert_out.astype(jnp.bfloat16).reshape(-1, capacity, features)
    returned = lax.all_to_all(
        expert_low, "expert", split_axis=0, concat_axis=0, tiled=True
    ).reshape(experts * capacity, features)
    picked = jnp.take(returned, token_flat, axis=0, mode="fill", fill_value=0).astype(jnp.float32)
    block_output = (residual + jnp.sum(chosen[:, :, None] * picked, axis=1)).astype(jnp.bfloat16)
    grad_float = out_grad.astype(jnp.float32)
    gate_grad = jnp.sum(grad_float[:, None, :] * picked, axis=2)
    pair_grad = (chosen[:, :, None] * grad_float[:, None, :]).astype(jnp.bfloat16)
    slot_grad = (
        jnp.zeros((experts * capacity, features), jnp.bfloat16)
        .at[token_flat.reshape(-1)]
        .set(pair_grad.reshape(-1, features), mode="drop")
    )
    grad_arrived = lax.all_to_all(
        slot_grad.reshape(experts, capacity, features),
        "expert",
        split_axis=0,
        concat_axis=0,
        tiled=True,
    )
    grad_rows = grad_arrived.reshape(-1, local_experts, capacity, features)
    hidden_grad = jnp.einsum(
        "secd,efd->secf", grad_rows, down_weight, preferred_element_type=jnp.float32
    )
    (inner_grad,) = gelu_back(hidden_grad)
    inner_low = inner_grad.astype(jnp.bfloat16)
    rows_grad = jnp.einsum(
        "secf,edf->secd", inner_low, up_weight, preferred_element_type=jnp.float32
    ).astype(jnp.bfloat16)
    rows_back = lax.all_to_all(
        rows_grad.reshape(-1, capacity, features), "expert", split_axis=0, concat_axis=0, tiled=True
    ).reshape(experts * capacity, features)
    up_local = jnp.einsum(
        "secd,secf->edf", arrived_rows, inner_low, preferred_element_type=jnp.float32
    )
    down_local = jnp.einsum(
        "secf,secd->efd", hidden_low, grad_rows, preferred_element_type=jnp.float32
    )
    up_bias_local = jnp.sum(inner_low, axis=(0, 2), dtype=jnp.float32)
    down_bias_local = jnp.sum(grad_rows, axis=(0, 2), dtype=jnp.float32)
    up_grad, down_grad, up_bias_grad, down_bias_grad = (
        lax.psum_scatter(
            up_local.astype(jnp.bfloat16), "dp", scatter_dimension=2, tiled=True
        ).astype(jnp.float32),
        lax.psum_scatter(
            down_local.astype(jnp.bfloat16), "dp", scatter_dimension=1, tiled=True
        ).astype(jnp.float32),
        lax.psum_scatter(
            up_bias_local.astype(jnp.bfloat16), "dp", scatter_dimension=1, tiled=True
        ).astype(jnp.float32),
        lax.psum_scatter(
            down_bias_local.astype(jnp.bfloat16), "dp", scatter_dimension=1, tiled=True
        ).astype(jnp.float32),
    )
    joint_back, out_back, router_back = (
        lax.all_gather(joint_weight, "expert", axis=0, tiled=True),
        lax.all_gather(out_weight, "expert", axis=0, tiled=True),
        lax.all_gather(router_weight, "expert", axis=0, tiled=True),
    )
    expert_iota = jnp.arange(experts, dtype=jnp.int32)
    choice_hot = (expert_ids[:, :, None] == expert_iota[None, None, :]).astype(jnp.float32)
    mass_grad = jnp.sum(gate_grad[:, :, None] * choice_hot, axis=1)
    logit_grad = (
        gate_weights * (mass_grad - jnp.sum(gate_weights * mass_grad, axis=1, keepdims=True))
    ).astype(jnp.bfloat16)
    router_local = jnp.einsum("td,te->de", two_low, logit_grad, preferred_element_type=jnp.float32)
    two_grad = jnp.einsum("te,de->td", logit_grad, router_back, preferred_element_type=jnp.float32)
    two_grad = two_grad + jnp.sum(
        jnp.take(rows_back, token_flat, axis=0, mode="fill", fill_value=0).astype(jnp.float32),
        axis=1,
    )
    residual_part, gain_two, shift_two = norm_two_back(two_grad)
    residual_grad = grad_float + residual_part
    branch_low = residual_grad.astype(jnp.bfloat16)
    out_local = jnp.einsum(
        "td,te->de", attended_low, branch_low, preferred_element_type=jnp.float32
    )
    attended_grad = jnp.einsum(
        "te,de->td", branch_low, out_back, preferred_element_type=jnp.float32
    )
    attended_grad = attended_grad.astype(jnp.bfloat16).reshape(images, SEQ, HEADS, HEAD_DIM)
    scores_again = (
        jnp.einsum("ishd,ithd->ihst", query_heads, key_heads, preferred_element_type=jnp.float32)
        * head_scale
    )
    weighting_again = jnp.exp(scores_again - log_total)
    weight_grad = jnp.einsum(
        "ishd,ithd->ihst", attended_grad, value_heads, preferred_element_type=jnp.float32
    )
    value_grad = jnp.einsum(
        "ihst,ishd->ithd",
        weighting_again.astype(jnp.bfloat16),
        attended_grad,
        preferred_element_type=jnp.float32,
    )
    score_grad = (
        weighting_again
        * (weight_grad - jnp.sum(weight_grad * weighting_again, axis=-1, keepdims=True))
    ).astype(jnp.bfloat16)
    query_grad = (
        jnp.einsum("ihst,ithd->ishd", score_grad, key_heads, preferred_element_type=jnp.float32)
        * head_scale
    )
    key_grad = (
        jnp.einsum("ihst,ishd->ithd", score_grad, query_heads, preferred_element_type=jnp.float32)
        * head_scale
    )
    projected_grad = (
        jnp.stack([query_grad, key_grad, value_grad], axis=2)
        .reshape(row_count, 3 * features)
        .astype(jnp.bfloat16)
    )
    joint_local = jnp.einsum(
        "td,te->de", normed_low, projected_grad, preferred_element_type=jnp.float32
    )
    bias_sums = jnp.sum(projected_grad, axis=0, dtype=jnp.float32)
    normed_grad = jnp.einsum(
        "te,de->td", projected_grad, joint_back, preferred_element_type=jnp.float32
    )
    input_part, gain_one, shift_one = norm_back(normed_grad)
    input_grad = (residual_grad + input_part).astype(jnp.bfloat16)
    gains_local = jnp.stack([gain_one, gain_two])
    shifts_local = jnp.stack([shift_one, shift_two])
    bias_local = jnp.stack(
        [bias_sums[:features], bias_sums[2 * features :], jnp.sum(residual_grad, axis=0)]
    )
    joint_part, out_part, router_part, gains_part, shifts_part, bias_part = (
        lax.psum_scatter(
            joint_local.astype(jnp.bfloat16), "expert", scatter_dimension=0, tiled=True
        ).astype(jnp.float32),
        lax.psum_scatter(
            out_local.astype(jnp.bfloat16), "expert", scatter_dimension=0, tiled=True
        ).astype(jnp.float32),
        lax.psum_scatter(
            router_local.astype(jnp.bfloat16), "expert", scatter_dimension=0, tiled=True
        ).astype(jnp.float32),
        lax.psum_scatter(
            gains_local.astype(jnp.bfloat16), "expert", scatter_dimension=1, tiled=True
        ).astype(jnp.float32),
        lax.psum_scatter(
            shifts_local.astype(jnp.bfloat16), "expert", scatter_dimension=1, tiled=True
        ).astype(jnp.float32),
        lax.psum_scatter(
            bias_local.astype(jnp.bfloat16), "expert", scatter_dimension=1, tiled=True
        ).astype(jnp.float32),
    )
    joint_grad, out_weight_grad, router_grad, gains_grad, shifts_grad, attention_bias_grad = (
        lax.psum(joint_part.astype(jnp.bfloat16), "dp").astype(jnp.float32),
        lax.psum(out_part.astype(jnp.bfloat16), "dp").astype(jnp.float32),
        lax.psum(router_part.astype(jnp.bfloat16), "dp").astype(jnp.float32),
        lax.psum(gains_part.astype(jnp.bfloat16), "dp").astype(jnp.float32),
        lax.psum(shifts_part.astype(jnp.bfloat16), "dp").astype(jnp.float32),
        lax.psum(bias_part.astype(jnp.bfloat16), "dp").astype(jnp.float32),
    )
    return (
        block_output,
        input_grad,
        joint_grad,
        out_weight_grad,
        router_grad,
        gains_grad,
        shifts_grad,
        attention_bias_grad,
        up_grad,
        down_grad,
        up_bias_grad,
        down_bias_grad,
    )


def solution(mesh):
    in_specs = (
        P(("dp", "expert"), None),
        P(("dp", "expert"), None),
        P(("dp", "expert"), None),
        P(("dp", "expert"), None),
        P("expert", None),
        P("expert", None),
        P("expert", None),
        P(None, "expert"),
        P(None, "expert"),
        P(None, "expert"),
        P("expert", None, None),
        P("expert", None, None),
        P("expert", None),
        P("expert", None),
    )
    out_specs = (
        P(("dp", "expert"), None),
        P(("dp", "expert"), None),
        P("expert", None),
        P("expert", None),
        P("expert", None),
        P(None, "expert"),
        P(None, "expert"),
        P(None, "expert"),
        P("expert", None, "dp"),
        P("expert", "dp", None),
        P("expert", "dp"),
        P("expert", "dp"),
    )
    return jax.shard_map(
        per_device, mesh=mesh, in_specs=in_specs, out_specs=out_specs, check_vma=False
    )
```

profile of v0, /device:TPU:0, one launch (start us, length us, event | category | flops | bytes accessed | tf_op | source)
XLA Modules:
  0.0 785.0 jit_solution(7141210550305157832)
XLA Ops:
  14.9 1.5 scatter_custom_fusion
  16.8 5.3 scatter_custom_fusion.1
  23.2 10.3 %all-gather = bf16[8,96,2]{1,2,0:T(2,128)(2,1)S(1)} all-gather(bf16[1,96,2]{1,2,0:T(2,128)(2,1)S(1)} %bitcast.274), channel_id=1, replica_groups=mesh['dp'=4,'expert'=8] {'expert'}, dimensions={0}, use_global_device_ids=true | all-gather | bytes 3456 | tf_op jit(solution)/shard_map/all_gather | solution.py:70
  33.6 9.2 %all-gather.2 = bf16[8,96,3]{1,2,0:T(4,128)(2,1)S(1)} all-gather(bf16[1,96,3]{1,2,0:T(4,128)(2,1)S(1)} %bitcast.273), channel_id=1, replica_groups=mesh['dp'=4,'expert'=8] {'expert'}, dimensions={0}, use_global_device_ids=true | all-gather | bytes 5184 | tf_op jit(solution)/shard_map/all_gather | solution.py:72
  42.9 7.8 all-gather.1
  51.0 3.7 fusion.36
  54.8 4.9 reshape.440
  59.8 5.0 fusion.123
  64.7 1.6 copy.210
  66.4 2.5 copy.211
  68.9 2.5 copy.209
  77.1 2.3 fusion.126
  80.7 5.2 gather_fusion.1
  85.9 1.5 gather.20
  88.8 4.4 all-to-all-start
  93.3 24.0 %all-gather.3 = bf16[8,96,8]{1,2,0:T(8,128)(2,1)S(1)} all-gather(bf16[1,96,8]{1,2,0:T(8,128)(2,1)S(1)} %bitcast.272), channel_id=1, replica_groups=mesh['dp'=4,'expert'=8] {'expert'}, dimensions={0}, use_global_device_ids=true | all-gather | bytes 13824 | tf_op jit(solution)/shard_map/all_gather | solution.py:69
  117.7 2.1 mul.253
  119.8 3.3 mul.261
  123.5 8.1 %gather_fusion.2 = f32[788]{0:T(1024)S(1)} fusion(f32[394,8]{0,1:T(8,128)S(1)} %fusion.99, s32[788]{0:T(1024)S(1)} %reshape.365), kind=kCustom, calls=%fused_computation.4 | custom fusion | bytes 12608 | tf_op jit(solution)/shard_map/jit(take_along_axis)/gather | solution.py:119
  132.2 8.8 %scatter_custom_fusion.2 = bf16[992,768]{1,0:T(8,128)(2,1)} fusion(s32[788]{0:T(1024)S(1)} %fusion.101, f32[788,768]{1,0:T(8,128)S(1)} %mul.261, f32[788]{0:T(1024)S(1)} %mul.259, bf16[]{:T(256)} %constant.104.clone.1), kind=kCustom, calls=%fused_computation.104 | custom fusion | flops 1210368 | bytes 3960834 | tf_op jit(solution)/shard_map/scatter | solution.py:148
  141.0 2.4 reshape.321
  143.4 3.9 all-to-all-start.2
  147.4 10.0 %fusion.27 = f32[8,124,3072]{2,1,0:T(8,128)} fusion(bf16[8,124,768]{2,1,0:T(8,128)(2,1)} %all-to-all-done, bf16[1,768,3072]{2,1,0:T(8,128)(2,1)} %param.26), kind=kOutput, calls=%fused_computation.46 | convolution fusion | flops 4680843264 | bytes 18432000 | tf_op jit(solution)/shard_map/secd,edf->secf/dot_general | solution.py:127
  157.4 10.9 %all-to-all-done.2 = bf16[8,124,768]{2,1,0:T(8,128)(2,1)S(1)} async-done(((bf16[8,124,768]{2,1,0:T(8,128)(2,1)}), bf16[8,124,768]{2,1,0:T(8,128)(2,1)S(1)}, u32[]{:S(2)}, u32[]{:S(2)}) %all-to-all-start.2) | async-done | bytes 1523744 | tf_op jit(solution)/shard_map/all_to_all | solution.py:150
  168.3 15.5 %fusion.128 = (bf16[3072]{0:T(1024)(128)(2,1)S(1)}, bf16[8,1,124,3072]{3,2,0,1:T(8,128)(2,1)S(1)}) fusion(f32[3072]{0:T(1024)S(1)} %bitcast.264, f32[8,124,3072]{2,1,0:T(8,128)} %fusion.27, bf16[8,124,768]{2,1,0:T(8,128)(2,1)S(1)} %all-to-all-done.2, bf16[1,3072,768]{2,1,0:T(8,128)(2,1)} %param.27), kind=kOutput, calls=%fused_computation.213 | convolution fusion | flops 4747883520 | bytes 24545280 | tf_op jit(solution)/shard_map/secd,efd->secf/dot_general | solution.py:158
  183.8 2.6 copy-done.51
  186.4 8.5 %fusion.56 = bf16[8,124,768]{2,1,0:T(8,128)(2,1)} fusion(bf16[1,768,3072]{2,1,0:T(8,128)(2,1)} %param.26, bf16[8,1,124,3072]{3,2,0,1:T(8,128)(2,1)S(1)} %get-tuple-element.63), kind=kOutput, calls=%fused_computation.78 | convolution fusion | flops 4681605120 | bytes 12337152 | tf_op jit(solution)/shard_map/secf,edf->secd/dot_general | solution.py:163
  194.9 3.6 all-to-all-start.3
  198.5 13.0 %fusion.61 = bf16[8,124,768]{2,1,0:T(8,128)(2,1)} fusion(f32[768]{0:T(1024)S(1)} %convert_reduce_fusion.3, bf16[1,3072,768]{2,1,0:T(8,128)(2,1)} %param.27, f32[8,124,3072]{2,1,0:T(8,128)} %fusion.27, f32[3072]{0:T(1024)S(1)} %bitcast.265), kind=kOutput, calls=%fused_computation.83 | convolution fusion | flops 4712841216 | bytes 18447360 | tf_op jit(solution)/shard_map/secf,efd->secd/dot_general | solution.py:133
  211.5 8.0 %all-to-all-done.3 = bf16[8,124,768]{2,1,0:T(8,128)(2,1)S(1)} async-done(((bf16[8,124,768]{2,1,0:T(8,128)(2,1)}), bf16[8,124,768]{2,1,0:T(8,128)(2,1)S(1)}, u32[]{:S(2)}, u32[]{:S(2)}) %all-to-all-start.3) | async-done | bytes 1523744 | tf_op jit(solution)/shard_map/all_to_all | solution.py:166
  219.5 4.3 all-to-all-start.1
  226.0 3.7 gather_fusion.4
  229.7 1.9 reshape.423
  231.6 13.2 %all-to-all-done.1 = bf16[8,124,768]{2,1,0:T(8,128)(2,1)} async-done(((bf16[8,124,768]{2,1,0:T(8,128)(2,1)}), bf16[8,124,768]{2,1,0:T(8,128)(2,1)}, u32[]{:S(2)}, u32[]{:S(2)}) %all-to-all-start.1) | async-done | bytes 1523744 | tf_op jit(solution)/shard_map/all_to_all | solution.py:137
  244.8 1.5 reshape.320
  246.3 3.7 gather_fusion.3
  250.0 1.9 reshape.419
  251.9 15.9 %fusion.47 = (f32[394,2]{1,0:T(8,128)S(1)}, f32[394,768]{1,0:T(8,128)}, f32[394,768]{1,0:T(8,128)S(1)}) fusion(f32[394,768]{1,0:T(8,128)} %convert_element_type.195, bf16[394,2,768]{2,1,0:T(2,128)(2,1)} %reshape.419, pred[394,2]{1,0:T(8,128)(4,1)S(1)} %compare_and_fusion, f32[394,2]{1,0:T(8,128)S(1)} %copy.171, bf16[394,2,768]{2,1,0:T(2,128)(2,1)} %reshape.423), kind=kLoop, calls=%fused_computation.65 | loop fusion | flops 4840684 | bytes 6058932 | tf_op jit(solution)/shard_map/reduce_sum | solution.py:143
  269.4 1.4 fusion.122
  270.8 1.9 convolution_convert_fusion.1
  272.7 2.0 convolution_convert_fusion.2
  278.0 3.9 multiply_reduce_fusion
  281.9 3.8 multiply_convert_fusion.1
  289.5 3.9 copy.184
  293.4 6.6 convert_element_type.206
  300.0 5.8 convolution_convert_fusion
  310.1 5.0 fusion.120
  316.4 1.5 fusion.119
  322.0 42.4 %reduce-scatter.23.cloned.1.call-done = bf16[96,2304]{1,0:T(8,128)(2,1)} async-done(((bf16[768,2304]{1,0:T(8,128)(2,1)}), bf16[96,2304]{1,0:T(8,128)(2,1)}) %reduce-scatter.23.cloned.1.call-update) | async-done | bytes 442384 | tf_op jit(solution)/shard_map/reduce_scatter | solution.py:264
  364.5 12.2 %fusion.32 = bf16[1,3072,768]{2,1,0:T(8,128)(2,1)} fusion(bf16[8,124,768]{2,1,0:T(8,128)(2,1)S(1)} %copy-done.12, f32[8,124,3072]{2,1,0:T(8,128)} %fusion.27, f32[3072]{0:T(1024)S(1)} %bitcast.266), kind=kOutput, calls=%fused_computation.49 | convolution fusion | flops 4713676800 | bytes 18444288 | tf_op jit(solution)/shard_map/secf,secd->efd/dot_general | solution.py:172
  376.7 9.1 %fusion.29 = bf16[1,768,3072]{2,1,0:T(8,128)(2,1)} fusion(bf16[8,124,768]{2,1,0:T(8,128)(2,1)} %all-to-all-done, bf16[8,1,124,3072]{3,2,0,1:T(8,128)(2,1)} %copy-done.51), kind=kOutput, calls=%fused_computation.48 | convolution fusion | flops 4683202560 | bytes 12337152 | tf_op jit(solution)/shard_map/secd,secf->edf/dot_general | solution.py:169
  387.6 22.7 %reduce-scatter.39.cloned.1.call-done = bf16[768,1]{1,0:T(8,128)(2,1)} async-done(((bf16[3072,1]{1,0:T(8,128)(2,1)}), bf16[768,1]{1,0:T(8,128)(2,1)}) %reduce-scatter.39.cloned.1.call-update) | async-done | bytes 1552
  412.0 35.1 %reduce-scatter.35.cloned.1.call-done = bf16[96,2]{1,0:T(8,128)(2,1)} async-done(((bf16[768,2]{1,0:T(8,128)(2,1)}), bf16[96,2]{1,0:T(8,128)(2,1)}) %reduce-scatter.35.cloned.1.call-update) | async-done | bytes 400
  447.9 36.4 %reduce-scatter.33.cloned.1.call-done = bf16[96,2]{1,0:T(8,128)(2,1)} async-done(((bf16[768,2]{1,0:T(8,128)(2,1)}), bf16[96,2]{1,0:T(8,128)(2,1)}) %reduce-scatter.33.cloned.1.call-update) | async-done | bytes 400
  485.1 35.9 %reduce-scatter.37.cloned.1.call-done = bf16[96,3]{1,0:T(8,128)(2,1)} async-done(((bf16[768,3]{1,0:T(8,128)(2,1)}), bf16[96,3]{1,0:T(8,128)(2,1)}) %reduce-scatter.37.cloned.1.call-update) | async-done | bytes 592
  521.8 36.3 %reduce-scatter.31.cloned.1.call-done = bf16[96,8]{1,0:T(8,128)(2,1)} async-done(((bf16[768,8]{1,0:T(8,128)(2,1)}), bf16[96,8]{1,0:T(8,128)(2,1)}) %reduce-scatter.31.cloned.1.call-update) | async-done | bytes 1552
  558.9 11.7 %all-reduce.2 = (bf16[96,8]{0,1:T(8,128)(2,1)S(1)}, bf16[2,96]{1,0:T(2,128)(2,1)S(1)}, bf16[2,96]{1,0:T(2,128)(2,1)S(1)}, bf16[3,96]{1,0:T(4,128)(2,1)S(1)}) all-reduce(bf16[96,8]{0,1:T(8,128)(2,1)S(1)} %copy.194, bf16[2,96]{1,0:T(2,128)(2,1)S(1)} %copy.196, ...), channel_id=1, replica_groups=mesh['dp'=4,'expert'=8] {'dp'}, use_global_device_ids=true, to_apply=%region_33.35 | all-reduce | flops 1440 | bytes 5760 | tf_op jit(solution)/shard_map/psum | solution.py:286
  572.9 27.4 %all-reduce.6.cloned.1.call-done = (bf16[96,2304]{1,0:T(8,128)(2,1)}, bf16[96,768]{1,0:T(8,128)(2,1)}) async-done(((bf16[96,2304]{1,0:T(8,128)(2,1)}, bf16[96,768]{1,0:T(8,128)(2,1)}), (bf16[96,2304]{1,0:T(8,128)(2,1)}, bf16[96,768]{1,0:T(8,128)(2,1)})) %all-reduce.6.cloned.1.call-update) | async-done | bytes 589840 | tf_op jit(solution)/shard_map/psum | solution.py:284
  600.3 2.0 convert_element_type.209
  602.3 1.6 convert_element_type.211
  603.9 83.3 %reduce-scatter.29.cloned.1.call-done = bf16[1,768,768]{2,1,0:T(8,128)(2,1)} async-done(((bf16[1,3072,768]{2,1,0:T(8,128)(2,1)}), bf16[1,768,768]{2,1,0:T(8,128)(2,1)}) %reduce-scatter.29.cloned.1.call-update) | async-done | bytes 1179664 | tf_op jit(solution)/shard_map/reduce_scatter | solution.py:181
  687.2 2.8 convert_element_type.223
  690.1 85.3 %reduce-scatter.27.cloned.1.call-done = bf16[1,768,768]{2,1,0:T(8,128)(2,1)} async-done(((bf16[1,768,3072]{2,1,0:T(8,128)(2,1)}), bf16[1,768,768]{2,1,0:T(8,128)(2,1)}) %reduce-scatter.27.cloned.1.call-update) | async-done | bytes 1179664 | tf_op jit(solution)/shard_map/reduce_scatter | solution.py:178
  775.4 2.8 convert_element_type.220
  (267 shorter events, 48.2 us)
Async XLA Ops:
  7.2 4.3 copy-start.43
  7.2 43.8 %all-gather.7.cloned.1.call-start = ((), (), s32[]{:S(2)}) async-start(), calls=%async_computation.14 | async-start | bytes 3981312 | tf_op jit(solution)/shard_map/all_gather | solution.py:67
  7.9 69.1 %all-gather.9.cloned.1.call-start = ((), (), s32[]{:S(2)}) async-start(), calls=%async_computation.15 | async-start | bytes 1327104 | tf_op jit(solution)/shard_map/all_gather | solution.py:68
  10.2 11.9 %copy-start.5 = (bf16[394,768]{1,0:T(8,128)(2,1)S(1)}, bf16[394,768]{1,0:T(8,128)(2,1)}, u32[]{:S(2)}) copy-start(bf16[394,768]{1,0:T(8,128)(2,1)} %param.16) | copy-start | bytes 1815556
  11.3 11.8 %copy-start.49 = (bf16[2,96]{1,0:T(2,128)(2,1)S(1)}, bf16[2,96]{1,0:T(2,128)(2,1)}, u32[]{:S(2)}) copy-start(bf16[2,96]{1,0:T(2,128)(2,1)} %param.23) | copy-start | bytes 1156
  11.4 22.2 %copy-start.48 = (bf16[3,96]{1,0:T(4,128)(2,1)S(1)}, bf16[3,96]{1,0:T(4,128)(2,1)}, u32[]{:S(2)}) copy-start(bf16[3,96]{1,0:T(4,128)(2,1)} %param.25) | copy-start | bytes 1732
  11.4 31.6 %copy-start.50 = (bf16[2,96]{1,0:T(2,128)(2,1)S(1)}, bf16[2,96]{1,0:T(2,128)(2,1)}, u32[]{:S(2)}) copy-start(bf16[2,96]{1,0:T(2,128)(2,1)} %param.24) | copy-start | bytes 1156
  16.4 38.3 %copy-start.19 = (s32[394,2]{1,0:T(8,128)}, s32[394,2]{1,0:T(8,128)S(1)}, u32[]{:S(2)}) copy-start(s32[394,2]{1,0:T(8,128)S(1)} %scatter_custom_fusion) | copy-start | bytes 9460
  22.3 32.5 %copy-start.34 = (f32[394]{0:T(512)}, f32[394]{0:T(512)S(1)}, u32[]{:S(2)}) copy-start(f32[394]{0:T(512)S(1)} %broadcast_multiply_fusion.1) | copy-start | bytes 4732
  22.6 32.2 %copy-start.40 = (f32[394]{0:T(512)}, f32[394]{0:T(512)S(1)}, u32[]{:S(2)}) copy-start(f32[394]{0:T(512)S(1)} %fusion.104) | copy-start | bytes 4732
  33.5 21.3 %copy-start.30 = (f32[768]{0:T(1024)}, f32[768]{0:T(1024)S(1)}, u32[]{:S(2)}) copy-start(f32[768]{0:T(1024)S(1)} %get-tuple-element.27) | copy-start | bytes 9220
  33.6 46.2 %copy-start.25 = (f32[768]{0:T(1024)}, f32[768]{0:T(1024)S(1)}, u32[]{:S(2)}) copy-start(f32[768]{0:T(1024)S(1)} %get-tuple-element.26) | copy-start | bytes 9220
  50.9 4.0 copy-start.44
  66.4 5.0 copy-start.7
  68.9 3.4 copy-start.9
  71.4 1.9 copy-start.21
  72.3 2.2 copy-start.2
  77.0 2.4 copy-start.23
  79.4 6.5 copy-start.28
  79.7 6.2 copy-start.38
  79.7 6.2 copy-start.32
  80.7 42.4 %copy-start = (bf16[394,768]{1,0:T(8,128)(2,1)}, bf16[394,768]{1,0:T(8,128)(2,1)S(1)}, u32[]{:S(2)}) copy-start(bf16[394,768]{1,0:T(8,128)(2,1)S(1)} %add_convert_fusion.2) | copy-start | bytes 1815556
  88.8 4.5 copy-start.47
  88.8 28.6 %copy-start.27 = (s32[394,2]{0,1:T(2,128)S(1)}, s32[394,2]{0,1:T(2,128)}, u32[]{:S(2)}) copy-start(s32[394,2]{0,1:T(2,128)} %param.18) | copy-start | bytes 9460
  88.8 28.9 %copy-start.13 = (bf16[394,768]{1,0:T(8,128)(2,1)S(1)}, bf16[394,768]{1,0:T(8,128)(2,1)}, u32[]{:S(2)}) copy-start(bf16[394,768]{1,0:T(8,128)(2,1)} %param.17) | copy-start | bytes 1815556
  88.8 54.6 %all-to-all-start = ((bf16[8,124,768]{2,1,0:T(8,128)(2,1)}), bf16[8,124,768]{2,1,0:T(8,128)(2,1)}, u32[]{:S(2)}, u32[]{:S(2)}) async-start(bf16[8,124,768]{2,1,0:T(8,128)(2,1)} %broadcast_select_fusion.2), calls=%async_computation | async-start | bytes 3145728 | tf_op jit(solution)/shard_map/all_to_all | solution.py:124
  143.4 4.0 copy-start.42
  143.4 4.0 copy-start.46
  143.4 24.9 %all-to-all-start.2 = ((bf16[8,124,768]{2,1,0:T(8,128)(2,1)}), bf16[8,124,768]{2,1,0:T(8,128)(2,1)S(1)}, u32[]{:S(2)}, u32[]{:S(2)}) async-start(bf16[8,124,768]{2,1,0:T(8,128)(2,1)} %reshape.321), calls=%async_computation.2 | async-start | bytes 3145728 | tf_op jit(solution)/shard_map/all_to_all | solution.py:150
  168.3 15.5 %copy-start.11 = (bf16[8,124,768]{2,1,0:T(8,128)(2,1)}, bf16[8,124,768]{2,1,0:T(8,128)(2,1)S(1)}, u32[]{:S(2)}) copy-start(bf16[8,124,768]{2,1,0:T(8,128)(2,1)S(1)} %all-to-all-done.2) | copy-start | bytes 4571140
  183.8 2.6 copy-start.51
  194.9 24.5 %all-to-all-start.3 = ((bf16[8,124,768]{2,1,0:T(8,128)(2,1)}), bf16[8,124,768]{2,1,0:T(8,128)(2,1)S(1)}, u32[]{:S(2)}, u32[]{:S(2)}) async-start(bf16[8,124,768]{2,1,0:T(8,128)(2,1)} %fusion.56), calls=%async_computation.3 | async-start | bytes 3145728 | tf_op jit(solution)/shard_map/all_to_all | solution.py:166
  211.5 12.3 %copy-start.14 = (bf16[394,768]{1,0:T(8,128)(2,1)S(1)}, bf16[394,768]{1,0:T(8,128)(2,1)}, u32[]{:S(2)}) copy-start(bf16[394,768]{1,0:T(8,128)(2,1)} %param.17) | copy-start | bytes 1815556
  219.5 25.3 %all-to-all-start.1 = ((bf16[8,124,768]{2,1,0:T(8,128)(2,1)}), bf16[8,124,768]{2,1,0:T(8,128)(2,1)}, u32[]{:S(2)}, u32[]{:S(2)}) async-start(bf16[8,124,768]{2,1,0:T(8,128)(2,1)} %fusion.61), calls=%async_computation.1 | async-start | bytes 3145728 | tf_op jit(solution)/shard_map/all_to_all | solution.py:137
  223.8 98.2 %reduce-scatter.25.cloned.1.call-start = ((), (), s32[]{:S(2)}) async-start(), calls=%async_computation.17 | async-start | bytes 1327104 | tf_op jit(solution)/shard_map/reduce_scatter | solution.py:267
  251.9 16.1 %copy-start.4 = (f32[394,768]{1,0:T(8,128)S(1)}, f32[394,768]{1,0:T(8,128)}, u32[]{:S(2)}) copy-start(f32[394,768]{1,0:T(8,128)} %copy-done.3) | copy-start | bytes 3631108
  251.9 16.1 %copy-start.26 = (f32[768]{0:T(1024)S(1)}, f32[768]{0:T(1024)}, u32[]{:S(2)}) copy-start(f32[768]{0:T(1024)} %copy-done.25) | copy-start | bytes 9220
  251.9 16.1 %copy-start.29 = (f32[394]{0:T(512)S(1)}, f32[394]{0:T(512)}, u32[]{:S(2)}) copy-start(f32[394]{0:T(512)} %copy-done.28) | copy-start | bytes 4732
  251.9 16.1 %copy-start.33 = (f32[394]{0:T(512)S(1)}, f32[394]{0:T(512)}, u32[]{:S(2)}) copy-start(f32[394]{0:T(512)} %copy-done.32) | copy-start | bytes 4732
  268.1 1.3 copy-start.18
  269.4 1.4 copy-start.15
  269.4 1.4 copy-start.24
  270.7 2.0 copy-start.16
  276.9 87.5 %reduce-scatter.23.cloned.1.call-start = ((), (), s32[]{:S(2)}) async-start(), calls=%async_computation.16 | async-start | bytes 3981312 | tf_op jit(solution)/shard_map/reduce_scatter | solution.py:264
  278.0 9.9 %slice-start = ((s8[4915200]{0:T(1024)(128)(4,1)}), s8[4194304]{0:T(1024)(128)(4,1)S(1)}, s32[]{:S(2)}) async-start(s8[4915200]{0:T(1024)(128)(4,1)} %bitcast.247), calls=%async_computation.27 | async-start | bytes 8388608
  281.9 3.9 copy-start.10
  281.9 5.9 slice-start.1
  293.4 6.6 copy-start.6
  293.4 6.6 copy-start.31
  293.4 6.6 copy-start.35
  293.4 6.6 copy-start.41
  293.4 6.6 copy-start.45
  305.8 1.4 copy-start.12
  305.9 80.3 %reduce-scatter.41.cloned.1.call-start = ((), (), s32[]{:S(2)}) async-start(), calls=%async_computation.25 | async-start | bytes 245760
  308.4 101.9 %reduce-scatter.39.cloned.1.call-start = ((), (), s32[]{:S(2)}) async-start(), calls=%async_computation.24 | async-start | bytes 983040
  310.0 5.0 copy-start.37
  310.1 137.0 %reduce-scatter.35.cloned.1.call-start = ((), (), s32[]{:S(2)}) async-start(), calls=%async_computation.22 | async-start | bytes 221184
  316.4 4.5 copy-start.1
  318.8 165.5 %reduce-scatter.33.cloned.1.call-start = ((), (), s32[]{:S(2)}) async-start(), calls=%async_computation.21 | async-start | bytes 221184
  319.9 201.1 %reduce-scatter.37.cloned.1.call-start = ((), (), s32[]{:S(2)}) async-start(), calls=%async_computation.23 | async-start | bytes 221184
  320.8 237.3 %reduce-scatter.31.cloned.1.call-start = ((), (), s32[]{:S(2)}) async-start(), calls=%async_computation.20 | async-start | bytes 221184
  321.9 278.4 %all-reduce.6.cloned.1.call-start = ((), (), s32[]{:S(2)}) async-start(), calls=%async_computation.26 | async-start | bytes 1179648 | tf_op jit(solution)/shard_map/psum | solution.py:284
  364.4 322.8 %reduce-scatter.29.cloned.1.call-start = ((), (), s32[]{:S(2)}) async-start(), calls=%async_computation.19 | async-start | bytes 5898240 | tf_op jit(solution)/shard_map/reduce_scatter | solution.py:181
  376.7 398.7 %reduce-scatter.27.cloned.1.call-start = ((), (), s32[]{:S(2)}) async-start(), calls=%async_computation.18 | async-start | bytes 5898240 | tf_op jit(solution)/shard_map/reduce_scatter | solution.py:178
  (7 other events, 7.1 us)
Sparse Core Ops, SparseCore 0:
  9.9 36.5 all-gather.6
  48.4 23.9 all-gather.8
  277.0 36.0 reduce-scatter.24
  316.4 47.9 reduce-scatter.22
  366.5 19.5 reduce-scatter.40
  388.9 21.4 reduce-scatter.38
  413.9 33.1 reduce-scatter.34
  450.7 33.5 reduce-scatter.32
  487.3 33.6 reduce-scatter.36
  524.4 33.6 reduce-scatter.30
  560.5 39.7 all-reduce.5
  602.5 84.7 reduce-scatter.28
  689.5 85.7 reduce-scatter.26
where the time goes:
time: 794 us; the launch traced here: 785 us
  waiting for transfers between devices  439 us (55%)
  matrix products  98.8 us (12%)
  local copies, waits for them, and re-layouts  97.9 us (12%)
  blocking collectives  63 us (8%)
  other arithmetic  54.1 us (7%)
  starting transfers between devices  17.2 us (2%)
  between operations  15.3 us (2%)
    unnamed x19, waiting for transfers between devices  168 us
    reduce_scatter x1, waiting for transfers between devices, per_device(): lax.psum_scatter(up_local.astype(jnp.bfloat16), 'dp', scatter_dimension=2...  85.3 us
    reduce_scatter x1, waiting for transfers between devices, per_device(): lax.psum_scatter(down_local.astype(jnp.bfloat16), 'dp', scatter_dimension...  83.3 us
    reduce_scatter x1, waiting for transfers between devices, per_device(): lax.psum_scatter(joint_local.astype(jnp.bfloat16), 'expert', scatter_dime...  42.4 us
    psum x1, waiting for transfers between devices, per_device(): lax.psum(joint_part.astype(jnp.bfloat16), 'dp').astype(jnp.float32)  27.4 us
    unnamed x125, local copies, waits for them, and re-layouts  27.4 us
    all_gather x1, blocking collectives, per_device(): lax.all_gather(router_weight, 'expert', axis=0, tiled=True)  24 us
    reduce_sum x1, other arithmetic, per_device(): gate_grad = jnp.sum(grad_float[:, None, :] * picked, axis=2)  15.9 us
  transfers between devices with their start and end apart: 17, of which 13 were waited for; matrix products, arithmetic and copies ran while one was open for 22% of the time, Pallas kernels for 0%

commit v1 on v0

--- a/solution.py
+++ b/solution.py
@@ -281,7 +281,7 @@
         ).astype(jnp.float32),
     )
     joint_grad, out_weight_grad, router_grad, gains_grad, shifts_grad, attention_bias_grad = (
-        lax.psum(joint_part.astype(jnp.bfloat16), "dp").astype(jnp.float32),
+        jnp.sum(lax.all_gather(joint_part.astype(jnp.bfloat16), "dp"), axis=0).astype(jnp.float32),
         lax.psum(out_part.astype(jnp.bfloat16), "dp").astype(jnp.float32),
         lax.psum(router_part.astype(jnp.bfloat16), "dp").astype(jnp.float32),
         lax.psum(gains_part.astype(jnp.bfloat16), "dp").astype(jnp.float32),

time: 794 us -> 830 us (1.045)
  waiting for transfers between devices: 439 us -> 474 us
    all_gather x0 -> x1, waiting for transfers between devices: none -> 40.1 us  [per_device(): lax.all_gather(joint_part.astype(jnp.bfloat16), 'dp')]
    unnamed x19 -> x20, waiting for transfers between devices: 168 us -> 169 us
  transfers between devices with their start and end apart: 17 -> 18, of which waited for: 13 -> 14; matrix products, arithmetic and copies ran while one was open for 22% -> 21% of each run, Pallas kernels for 0% -> 0%
where the time goes in v1:
time: 830 us; the launch traced here: 821 us
  waiting for transfers between devices  474 us (57%)
  matrix products  98.8 us (12%)
  local copies, waits for them, and re-layouts  97.9 us (12%)
  blocking collectives  63 us (8%)
  other arithmetic  54.9 us (7%)
  starting transfers between devices  17.2 us (2%)
  between operations  15.3 us (2%)
    unnamed x20, waiting for transfers between devices  169 us
    reduce_scatter x1, waiting for transfers between devices, per_device(): lax.psum_scatter(up_local.astype(jnp.bfloat16), 'dp', scatter_dimension=2...  85.2 us
    reduce_scatter x1, waiting for transfers between devices, per_device(): lax.psum_scatter(down_local.astype(jnp.bfloat16), 'dp', scatter_dimension...  83.7 us
    reduce_scatter x1, waiting for transfers between devices, per_device(): lax.psum_scatter(joint_local.astype(jnp.bfloat16), 'expert', scatter_dime...  41.7 us
    all_gather x1, waiting for transfers between devices, per_device(): lax.all_gather(joint_part.astype(jnp.bfloat16), 'dp')  40.1 us
    unnamed x125, local copies, waits for them, and re-layouts  27.4 us
    all_gather x1, blocking collectives, per_device(): lax.all_gather(router_weight, 'expert', axis=0, tiled=True)  24 us
    psum x1, waiting for transfers between devices, per_device(): lax.psum(out_part.astype(jnp.bfloat16), 'dp').astype(jnp.float32)  22.1 us
  transfers between devices with their start and end apart: 18, of which 14 were waited for; matrix products, arithmetic and copies ran while one was open for 21% of the time, Pallas kernels for 0%

profile of v1, /device:TPU:0, one launch (start us, length us, event | category | flops | bytes accessed | tf_op | source)
XLA Modules:
  0.0 820.8 jit_solution(4943636292951089595)
XLA Ops:
  14.9 1.5 scatter_custom_fusion
  16.8 5.3 scatter_custom_fusion.1
  23.2 10.3 %all-gather.1 = bf16[8,96,2]{1,2,0:T(2,128)(2,1)S(1)} all-gather(bf16[1,96,2]{1,2,0:T(2,128)(2,1)S(1)} %bitcast.276), channel_id=1, replica_groups=mesh['dp'=4,'expert'=8] {'expert'}, dimensions={0}, use_global_device_ids=true | all-gather | bytes 3456 | tf_op jit(solution)/shard_map/all_gather | solution.py:70
  33.6 9.2 %all-gather.3 = bf16[8,96,3]{1,2,0:T(4,128)(2,1)S(1)} all-gather(bf16[1,96,3]{1,2,0:T(4,128)(2,1)S(1)} %bitcast.275), channel_id=1, replica_groups=mesh['dp'=4,'expert'=8] {'expert'}, dimensions={0}, use_global_device_ids=true | all-gather | bytes 5184 | tf_op jit(solution)/shard_map/all_gather | solution.py:72
  42.9 7.8 all-gather.2
  51.0 3.7 fusion.36
  54.8 4.9 reshape.441
  59.8 5.0 fusion.123
  64.7 1.6 copy.210
  66.4 2.5 copy.211
  68.9 2.5 copy.209
  77.1 2.3 fusion.126
  80.7 5.2 gather_fusion.1
  85.9 1.5 gather.20
  88.8 4.4 all-to-all-start
  93.3 24.0 %all-gather.4 = bf16[8,96,8]{1,2,0:T(8,128)(2,1)S(1)} all-gather(bf16[1,96,8]{1,2,0:T(8,128)(2,1)S(1)} %bitcast.274), channel_id=1, replica_groups=mesh['dp'=4,'expert'=8] {'expert'}, dimensions={0}, use_global_device_ids=true | all-gather | bytes 13824 | tf_op jit(solution)/shard_map/all_gather | solution.py:69
  117.7 2.1 mul.253
  119.8 3.3 mul.261
  123.5 8.1 gather_fusion.2
  132.2 8.8 %scatter_custom_fusion.2 = bf16[992,768]{1,0:T(8,128)(2,1)} fusion(s32[788]{0:T(1024)S(1)} %fusion.101, f32[788,768]{1,0:T(8,128)S(1)} %mul.261, f32[788]{0:T(1024)S(1)} %mul.259, bf16[]{:T(256)} %constant.105.clone.1), kind=kCustom, calls=%fused_computation.104 | custom fusion | flops 1210368 | bytes 3960834 | tf_op jit(solution)/shard_map/scatter | solution.py:148
  141.0 2.4 reshape.321
  143.4 3.9 all-to-all-start.2
  147.4 10.0 %fusion.27 = f32[8,124,3072]{2,1,0:T(8,128)} fusion(bf16[8,124,768]{2,1,0:T(8,128)(2,1)} %all-to-all-done, bf16[1,768,3072]{2,1,0:T(8,128)(2,1)} %param.26), kind=kOutput, calls=%fused_computation.46 | convolution fusion | flops 4680843264 | bytes 18432000 | tf_op jit(solution)/shard_map/secd,edf->secf/dot_general | solution.py:127
  157.4 10.9 %all-to-all-done.2 = bf16[8,124,768]{2,1,0:T(8,128)(2,1)S(1)} async-done(((bf16[8,124,768]{2,1,0:T(8,128)(2,1)}), bf16[8,124,768]{2,1,0:T(8,128)(2,1)S(1)}, u32[]{:S(2)}, u32[]{:S(2)}) %all-to-all-start.2) | async-done | bytes 1523744 | tf_op jit(solution)/shard_map/all_to_all | solution.py:150
  168.3 15.5 %fusion.128 = (bf16[3072]{0:T(1024)(128)(2,1)S(1)}, bf16[8,1,124,3072]{3,2,0,1:T(8,128)(2,1)S(1)}) fusion(f32[3072]{0:T(1024)S(1)} %bitcast.266, f32[8,124,3072]{2,1,0:T(8,128)} %fusion.27, bf16[8,124,768]{2,1,0:T(8,128)(2,1)S(1)} %all-to-all-done.2, bf16[1,3072,768]{2,1,0:T(8,128)(2,1)} %param.27), kind=kOutput, calls=%fused_computation.213 | convolution fusion | flops 4747883520 | bytes 24545280 | tf_op jit(solution)/shard_map/secd,efd->secf/dot_general | solution.py:158
  183.8 2.6 copy-done.51
  186.4 8.5 %fusion.56 = bf16[8,124,768]{2,1,0:T(8,128)(2,1)} fusion(bf16[1,768,3072]{2,1,0:T(8,128)(2,1)} %param.26, bf16[8,1,124,3072]{3,2,0,1:T(8,128)(2,1)S(1)} %get-tuple-element.61), kind=kOutput, calls=%fused_computation.78 | convolution fusion | flops 4681605120 | bytes 12337152 | tf_op jit(solution)/shard_map/secf,edf->secd/dot_general | solution.py:163
  194.9 3.6 all-to-all-start.3
  198.5 13.0 %fusion.61 = bf16[8,124,768]{2,1,0:T(8,128)(2,1)} fusion(f32[768]{0:T(1024)S(1)} %convert_reduce_fusion.3, bf16[1,3072,768]{2,1,0:T(8,128)(2,1)} %param.27, f32[8,124,3072]{2,1,0:T(8,128)} %fusion.27, f32[3072]{0:T(1024)S(1)} %bitcast.267), kind=kOutput, calls=%fused_computation.83 | convolution fusion | flops 4712841216 | bytes 18447360 | tf_op jit(solution)/shard_map/secf,efd->secd/dot_general | solution.py:133
  211.5 8.0 all-to-all-done.3
  219.5 4.3 all-to-all-start.1
  226.0 3.7 gather_fusion.4
  229.7 1.9 reshape.424
  231.6 13.2 %all-to-all-done.1 = bf16[8,124,768]{2,1,0:T(8,128)(2,1)} async-done(((bf16[8,124,768]{2,1,0:T(8,128)(2,1)}), bf16[8,124,768]{2,1,0:T(8,128)(2,1)}, u32[]{:S(2)}, u32[]{:S(2)}) %all-to-all-start.1) | async-done | bytes 1523744 | tf_op jit(solution)/shard_map/all_to_all | solution.py:137
  244.8 1.5 reshape.320
  246.3 3.7 gather_fusion.3
  250.0 1.9 reshape.420
  251.9 15.9 %fusion.47 = (f32[394,2]{1,0:T(8,128)S(1)}, f32[394,768]{1,0:T(8,128)}, f32[394,768]{1,0:T(8,128)S(1)}) fusion(f32[394,768]{1,0:T(8,128)} %convert_element_type.197, bf16[394,2,768]{2,1,0:T(2,128)(2,1)} %reshape.420, pred[394,2]{1,0:T(8,128)(4,1)S(1)} %compare_and_fusion, f32[394,2]{1,0:T(8,128)S(1)} %copy.171, bf16[394,2,768]{2,1,0:T(2,128)(2,1)} %reshape.424), kind=kLoop, calls=%fused_computation.65 | loop fusion | flops 4840684 | bytes 6058932 | tf_op jit(solution)/shard_map/reduce_sum | solution.py:143
  270.8 1.9 convolution_convert_fusion.1
  272.7 2.0 convolution_convert_fusion.2
  278.0 3.9 multiply_reduce_fusion
  281.9 3.8 multiply_convert_fusion.1
  289.5 3.9 copy.184
  293.4 6.6 convert_element_type.208
  300.0 5.8 convolution_convert_fusion
  310.1 5.0 fusion.120
  316.4 1.5 fusion.119
  322.7 41.7 %reduce-scatter.23.cloned.1.call-done = bf16[96,2304]{1,0:T(8,128)(2,1)} async-done(((bf16[768,2304]{1,0:T(8,128)(2,1)}), bf16[96,2304]{1,0:T(8,128)(2,1)}) %reduce-scatter.23.cloned.1.call-update) | async-done | bytes 442384 | tf_op jit(solution)/shard_map/reduce_scatter | solution.py:264
  364.5 12.2 %fusion.32 = bf16[1,3072,768]{2,1,0:T(8,128)(2,1)} fusion(bf16[8,124,768]{2,1,0:T(8,128)(2,1)S(1)} %copy-done.12, f32[8,124,3072]{2,1,0:T(8,128)} %fusion.27, f32[3072]{0:T(1024)S(1)} %bitcast.268), kind=kOutput, calls=%fused_computation.49 | convolution fusion | flops 4713676800 | bytes 18444288 | tf_op jit(solution)/shard_map/secf,secd->efd/dot_general | solution.py:172
  376.7 9.1 %fusion.29 = bf16[1,768,3072]{2,1,0:T(8,128)(2,1)} fusion(bf16[8,124,768]{2,1,0:T(8,128)(2,1)} %all-to-all-done, bf16[8,1,124,3072]{3,2,0,1:T(8,128)(2,1)} %copy-done.51), kind=kOutput, calls=%fused_computation.48 | convolution fusion | flops 4683202560 | bytes 12337152 | tf_op jit(solution)/shard_map/secd,secf->edf/dot_general | solution.py:169
  387.6 22.7 %reduce-scatter.39.cloned.1.call-done = bf16[768,1]{1,0:T(8,128)(2,1)} async-done(((bf16[3072,1]{1,0:T(8,128)(2,1)}), bf16[768,1]{1,0:T(8,128)(2,1)}) %reduce-scatter.39.cloned.1.call-update) | async-done | bytes 1552
  412.0 35.1 %reduce-scatter.35.cloned.1.call-done = bf16[96,2]{1,0:T(8,128)(2,1)} async-done(((bf16[768,2]{1,0:T(8,128)(2,1)}), bf16[96,2]{1,0:T(8,128)(2,1)}) %reduce-scatter.35.cloned.1.call-update) | async-done | bytes 400
  447.9 36.4 %reduce-scatter.33.cloned.1.call-done = bf16[96,2]{1,0:T(8,128)(2,1)} async-done(((bf16[768,2]{1,0:T(8,128)(2,1)}), bf16[96,2]{1,0:T(8,128)(2,1)}) %reduce-scatter.33.cloned.1.call-update) | async-done | bytes 400
  485.1 35.9 %reduce-scatter.37.cloned.1.call-done = bf16[96,3]{1,0:T(8,128)(2,1)} async-done(((bf16[768,3]{1,0:T(8,128)(2,1)}), bf16[96,3]{1,0:T(8,128)(2,1)}) %reduce-scatter.37.cloned.1.call-update) | async-done | bytes 592
  521.8 36.3 %reduce-scatter.31.cloned.1.call-done = bf16[96,8]{1,0:T(8,128)(2,1)} async-done(((bf16[768,8]{1,0:T(8,128)(2,1)}), bf16[96,8]{1,0:T(8,128)(2,1)}) %reduce-scatter.31.cloned.1.call-update) | async-done | bytes 1552
  558.9 11.7 %all-reduce.2 = (bf16[96,8]{0,1:T(8,128)(2,1)S(1)}, bf16[2,96]{1,0:T(2,128)(2,1)S(1)}, bf16[2,96]{1,0:T(2,128)(2,1)S(1)}, bf16[3,96]{1,0:T(4,128)(2,1)S(1)}) all-reduce(bf16[96,8]{0,1:T(8,128)(2,1)S(1)} %copy.194, bf16[2,96]{1,0:T(2,128)(2,1)S(1)} %copy.196, ...), channel_id=1, replica_groups=mesh['dp'=4,'expert'=8] {'dp'}, use_global_device_ids=true, to_apply=%region_33.35 | all-reduce | flops 1440 | bytes 5760 | tf_op jit(solution)/shard_map/psum | solution.py:286
  572.9 22.1 %all-reduce.5.cloned.1.call-done = bf16[96,768]{1,0:T(8,128)(2,1)} async-done(((bf16[96,768]{1,0:T(8,128)(2,1)}), bf16[96,768]{1,0:T(8,128)(2,1)}) %all-reduce.5.cloned.1.call-update) | async-done | bytes 147472 | tf_op jit(solution)/shard_map/psum | solution.py:285
  595.0 1.6 convert_element_type.213
  596.6 40.1 %all-gather.13.cloned.1.call-done = bf16[384,2304]{1,0:T(8,128)(2,1)} async-done(((bf16[96,2304]{1,0:T(8,128)(2,1)}), bf16[384,2304]{1,0:T(8,128)(2,1)}) %all-gather.13.cloned.1.call-update) | async-done | bytes 1769488 | tf_op jit(solution)/shard_map/all_gather | solution.py:284
  636.7 1.8 reduce_sum.316
  639.4 83.7 %reduce-scatter.29.cloned.1.call-done = bf16[1,768,768]{2,1,0:T(8,128)(2,1)} async-done(((bf16[1,3072,768]{2,1,0:T(8,128)(2,1)}), bf16[1,768,768]{2,1,0:T(8,128)(2,1)}) %reduce-scatter.29.cloned.1.call-update) | async-done | bytes 1179664 | tf_op jit(solution)/shard_map/reduce_scatter | solution.py:181
  723.1 2.8 convert_element_type.225
  726.0 85.2 %reduce-scatter.27.cloned.1.call-done = bf16[1,768,768]{2,1,0:T(8,128)(2,1)} async-done(((bf16[1,768,3072]{2,1,0:T(8,128)(2,1)}), bf16[1,768,768]{2,1,0:T(8,128)(2,1)}) %reduce-scatter.27.cloned.1.call-update) | async-done | bytes 1179664 | tf_op jit(solution)/shard_map/reduce_scatter | solution.py:178
  811.1 2.8 convert_element_type.222
  (271 shorter events, 51.2 us)
Async XLA Ops:
  7.2 4.3 copy-start.43
  7.2 43.8 %all-gather.9.cloned.1.call-start = ((), (), s32[]{:S(2)}) async-start(), calls=%async_computation.14 | async-start | bytes 3981312 | tf_op jit(solution)/shard_map/all_gather | solution.py:67
  7.9 69.1 %all-gather.11.cloned.1.call-start = ((), (), s32[]{:S(2)}) async-start(), calls=%async_computation.15 | async-start | bytes 1327104 | tf_op jit(solution)/shard_map/all_gather | solution.py:68
  10.2 11.9 %copy-start.5 = (bf16[394,768]{1,0:T(8,128)(2,1)S(1)}, bf16[394,768]{1,0:T(8,128)(2,1)}, u32[]{:S(2)}) copy-start(bf16[394,768]{1,0:T(8,128)(2,1)} %param.16) | copy-start | bytes 1815556
  11.3 11.8 %copy-start.49 = (bf16[2,96]{1,0:T(2,128)(2,1)S(1)}, bf16[2,96]{1,0:T(2,128)(2,1)}, u32[]{:S(2)}) copy-start(bf16[2,96]{1,0:T(2,128)(2,1)} %param.23) | copy-start | bytes 1156
  11.4 22.2 %copy-start.48 = (bf16[3,96]{1,0:T(4,128)(2,1)S(1)}, bf16[3,96]{1,0:T(4,128)(2,1)}, u32[]{:S(2)}) copy-start(bf16[3,96]{1,0:T(4,128)(2,1)} %param.25) | copy-start | bytes 1732
  11.4 31.6 %copy-start.50 = (bf16[2,96]{1,0:T(2,128)(2,1)S(1)}, bf16[2,96]{1,0:T(2,128)(2,1)}, u32[]{:S(2)}) copy-start(bf16[2,96]{1,0:T(2,128)(2,1)} %param.24) | copy-start | bytes 1156
  16.4 38.3 %copy-start.19 = (s32[394,2]{1,0:T(8,128)}, s32[394,2]{1,0:T(8,128)S(1)}, u32[]{:S(2)}) copy-start(s32[394,2]{1,0:T(8,128)S(1)} %scatter_custom_fusion) | copy-start | bytes 9460
  22.3 32.5 %copy-start.34 = (f32[394]{0:T(512)}, f32[394]{0:T(512)S(1)}, u32[]{:S(2)}) copy-start(f32[394]{0:T(512)S(1)} %broadcast_multiply_fusion.1) | copy-start | bytes 4732
  22.6 32.2 %copy-start.40 = (f32[394]{0:T(512)}, f32[394]{0:T(512)S(1)}, u32[]{:S(2)}) copy-start(f32[394]{0:T(512)S(1)} %fusion.104) | copy-start | bytes 4732
  33.5 21.3 %copy-start.30 = (f32[768]{0:T(1024)}, f32[768]{0:T(1024)S(1)}, u32[]{:S(2)}) copy-start(f32[768]{0:T(1024)S(1)} %get-tuple-element.27) | copy-start | bytes 9220
  33.6 46.2 %copy-start.25 = (f32[768]{0:T(1024)}, f32[768]{0:T(1024)S(1)}, u32[]{:S(2)}) copy-start(f32[768]{0:T(1024)S(1)} %get-tuple-element.26) | copy-start | bytes 9220
  50.9 4.0 copy-start.44
  66.4 5.0 copy-start.7
  68.9 3.4 copy-start.9
  71.4 1.9 copy-start.21
  72.3 2.2 copy-start.2
  77.0 2.4 copy-start.23
  79.4 6.5 copy-start.28
  79.7 6.2 copy-start.38
  79.7 6.2 copy-start.32
  80.7 42.4 %copy-start = (bf16[394,768]{1,0:T(8,128)(2,1)}, bf16[394,768]{1,0:T(8,128)(2,1)S(1)}, u32[]{:S(2)}) copy-start(bf16[394,768]{1,0:T(8,128)(2,1)S(1)} %add_convert_fusion.2) | copy-start | bytes 1815556
  88.8 4.5 copy-start.47
  88.8 28.6 %copy-start.27 = (s32[394,2]{0,1:T(2,128)S(1)}, s32[394,2]{0,1:T(2,128)}, u32[]{:S(2)}) copy-start(s32[394,2]{0,1:T(2,128)} %param.18) | copy-start | bytes 9460
  88.8 28.9 %copy-start.13 = (bf16[394,768]{1,0:T(8,128)(2,1)S(1)}, bf16[394,768]{1,0:T(8,128)(2,1)}, u32[]{:S(2)}) copy-start(bf16[394,768]{1,0:T(8,128)(2,1)} %param.17) | copy-start | bytes 1815556
  88.8 54.6 %all-to-all-start = ((bf16[8,124,768]{2,1,0:T(8,128)(2,1)}), bf16[8,124,768]{2,1,0:T(8,128)(2,1)}, u32[]{:S(2)}, u32[]{:S(2)}) async-start(bf16[8,124,768]{2,1,0:T(8,128)(2,1)} %broadcast_select_fusion.2), calls=%async_computation | async-start | bytes 3145728 | tf_op jit(solution)/shard_map/all_to_all | solution.py:124
  143.4 4.0 copy-start.42
  143.4 4.0 copy-start.46
  143.4 24.9 %all-to-all-start.2 = ((bf16[8,124,768]{2,1,0:T(8,128)(2,1)}), bf16[8,124,768]{2,1,0:T(8,128)(2,1)S(1)}, u32[]{:S(2)}, u32[]{:S(2)}) async-start(bf16[8,124,768]{2,1,0:T(8,128)(2,1)} %reshape.321), calls=%async_computation.2 | async-start | bytes 3145728 | tf_op jit(solution)/shard_map/all_to_all | solution.py:150
  168.3 15.5 %copy-start.11 = (bf16[8,124,768]{2,1,0:T(8,128)(2,1)}, bf16[8,124,768]{2,1,0:T(8,128)(2,1)S(1)}, u32[]{:S(2)}) copy-start(bf16[8,124,768]{2,1,0:T(8,128)(2,1)S(1)} %all-to-all-done.2) | copy-start | bytes 4571140
  183.8 2.6 copy-start.51
  194.9 24.5 %all-to-all-start.3 = ((bf16[8,124,768]{2,1,0:T(8,128)(2,1)}), bf16[8,124,768]{2,1,0:T(8,128)(2,1)S(1)}, u32[]{:S(2)}, u32[]{:S(2)}) async-start(bf16[8,124,768]{2,1,0:T(8,128)(2,1)} %fusion.56), calls=%async_computation.3 | async-start | bytes 3145728 | tf_op jit(solution)/shard_map/all_to_all | solution.py:166
  211.5 12.3 %copy-start.14 = (bf16[394,768]{1,0:T(8,128)(2,1)S(1)}, bf16[394,768]{1,0:T(8,128)(2,1)}, u32[]{:S(2)}) copy-start(bf16[394,768]{1,0:T(8,128)(2,1)} %param.17) | copy-start | bytes 1815556
  219.5 25.3 %all-to-all-start.1 = ((bf16[8,124,768]{2,1,0:T(8,128)(2,1)}), bf16[8,124,768]{2,1,0:T(8,128)(2,1)}, u32[]{:S(2)}, u32[]{:S(2)}) async-start(bf16[8,124,768]{2,1,0:T(8,128)(2,1)} %fusion.61), calls=%async_computation.1 | async-start | bytes 3145728 | tf_op jit(solution)/shard_map/all_to_all | solution.py:137
  223.8 98.2 %reduce-scatter.25.cloned.1.call-start = ((), (), s32[]{:S(2)}) async-start(), calls=%async_computation.17 | async-start | bytes 1327104 | tf_op jit(solution)/shard_map/reduce_scatter | solution.py:267
  251.9 16.1 %copy-start.4 = (f32[394,768]{1,0:T(8,128)S(1)}, f32[394,768]{1,0:T(8,128)}, u32[]{:S(2)}) copy-start(f32[394,768]{1,0:T(8,128)} %copy-done.3) | copy-start | bytes 3631108
  251.9 16.1 %copy-start.26 = (f32[768]{0:T(1024)S(1)}, f32[768]{0:T(1024)}, u32[]{:S(2)}) copy-start(f32[768]{0:T(1024)} %copy-done.25) | copy-start | bytes 9220
  251.9 16.1 %copy-start.29 = (f32[394]{0:T(512)S(1)}, f32[394]{0:T(512)}, u32[]{:S(2)}) copy-start(f32[394]{0:T(512)} %copy-done.28) | copy-start | bytes 4732
  251.9 16.1 %copy-start.33 = (f32[394]{0:T(512)S(1)}, f32[394]{0:T(512)}, u32[]{:S(2)}) copy-start(f32[394]{0:T(512)} %copy-done.32) | copy-start | bytes 4732
  269.4 1.4 copy-start.15
  269.4 1.4 copy-start.24
  270.7 2.0 copy-start.16
  276.9 87.5 %reduce-scatter.23.cloned.1.call-start = ((), (), s32[]{:S(2)}) async-start(), calls=%async_computation.16 | async-start | bytes 3981312 | tf_op jit(solution)/shard_map/reduce_scatter | solution.py:264
  278.0 9.9 %slice-start = ((s8[4915200]{0:T(1024)(128)(4,1)}), s8[4194304]{0:T(1024)(128)(4,1)S(1)}, s32[]{:S(2)}) async-start(s8[4915200]{0:T(1024)(128)(4,1)} %bitcast.248), calls=%async_computation.28 | async-start | bytes 8388608
  281.9 3.9 copy-start.10
  281.9 5.9 slice-start.1
  293.4 6.6 copy-start.6
  293.4 6.6 copy-start.31
  293.4 6.6 copy-start.35
  293.4 6.6 copy-start.41
  293.4 6.6 copy-start.45
  305.8 1.4 copy-start.12
  305.9 80.3 %reduce-scatter.41.cloned.1.call-start = ((), (), s32[]{:S(2)}) async-start(), calls=%async_computation.27 | async-start | bytes 245760
  308.4 101.9 %reduce-scatter.39.cloned.1.call-start = ((), (), s32[]{:S(2)}) async-start(), calls=%async_computation.26 | async-start | bytes 983040
  310.0 5.0 copy-start.37
  310.1 137.0 %reduce-scatter.35.cloned.1.call-start = ((), (), s32[]{:S(2)}) async-start(), calls=%async_computation.24 | async-start | bytes 221184
  316.4 4.5 copy-start.1
  318.8 165.5 %reduce-scatter.33.cloned.1.call-start = ((), (), s32[]{:S(2)}) async-start(), calls=%async_computation.23 | async-start | bytes 221184
  319.9 201.1 %reduce-scatter.37.cloned.1.call-start = ((), (), s32[]{:S(2)}) async-start(), calls=%async_computation.25 | async-start | bytes 221184
  320.8 237.3 %reduce-scatter.31.cloned.1.call-start = ((), (), s32[]{:S(2)}) async-start(), calls=%async_computation.22 | async-start | bytes 221184
  321.9 273.0 %all-reduce.5.cloned.1.call-start = ((), (), s32[]{:S(2)}) async-start(), calls=%async_computation.18 | async-start | bytes 294912 | tf_op jit(solution)/shard_map/psum | solution.py:285
  322.7 314.0 %all-gather.13.cloned.1.call-start = ((), (), s32[]{:S(2)}) async-start(), calls=%async_computation.21 | async-start | bytes 2211840 | tf_op jit(solution)/shard_map/all_gather | solution.py:284
  364.4 358.7 %reduce-scatter.29.cloned.1.call-start = ((), (), s32[]{:S(2)}) async-start(), calls=%async_computation.20 | async-start | bytes 5898240 | tf_op jit(solution)/shard_map/reduce_scatter | solution.py:181
  376.7 434.5 %reduce-scatter.27.cloned.1.call-start = ((), (), s32[]{:S(2)}) async-start(), calls=%async_computation.19 | async-start | bytes 5898240 | tf_op jit(solution)/shard_map/reduce_scatter | solution.py:178
  (8 other events, 8.4 us)
Sparse Core Ops, SparseCore 0:
  9.9 36.5 all-gather.8
  48.4 23.9 all-gather.10
  277.0 36.0 reduce-scatter.24
  316.4 47.9 reduce-scatter.22
  366.5 19.5 reduce-scatter.40
  388.9 21.4 reduce-scatter.38
  413.9 33.1 reduce-scatter.34
  450.7 33.5 reduce-scatter.32
  487.3 33.6 reduce-scatter.36
  524.4 33.6 reduce-scatter.30
  560.4 34.4 all-reduce.4
  596.4 40.2 all-gather.12
  639.0 84.1 reduce-scatter.28
  725.3 85.7 reduce-scatter.26
